TPU v7x, 256 devices: a whole 4x4x8 slice. The times are simulated.
256 devices in a mesh: gx: 8 (over x, core), gy: 4 (over z_lo), gz: 8 (over y, z_hi).
Axes of the slice: x: 4, y: 4, z: 8 (z_hi: 2, z_lo: 4; z = z_hi * 4 + z_lo), core: 2. Of those that a mesh axis runs over, the one named last changes fastest.
Arguments:
- start_block: float32 [32, 3, 2, 8, 16, 1024], P(None, None, None, 'gx', 'gy', 'gz'), may hold values from -700 to 700
- pair_blocks: float32 [3, 3, 16, 2, 8, 16, 1024], P(None, None, None, None, 'gx', 'gy', 'gz'), may hold values from -8 to 8, as said below
- slot_map: int32 [16, 2, 8, 16, 1024], P(None, None, 'gx', 'gy', 'gz'), may hold values from 0 to 15, as said below
Outputs:
- alpha1: float32 [32, 32], replicated
- alpha2: float32 [32, 32], replicated
- beta1: float32 [32, 32], replicated
- beta2: float32 [32, 32], replicated
- basis3: float32 [32, 3, 2, 8, 16, 1024], P(None, None, None, 'gx', 'gy', 'gz')
Inputs may be any that keep to these rules, and one draw needn't show every extreme that they name: `slot_map`: for every atom the 16 slots hold each of 0 to 15 once; 0 to 13 name the neighbour directions of the steps, 14 and 15 mark padding slots. `pair_blocks`: the block an atom holds toward a neighbour is the transpose of the block that neighbour holds toward the atom, so H is symmetric.
All inputs are finite; a program needn't handle non-finite values.
Results may differ from a plain program's by a relative error of at most 0.0003.
Values sent between devices are 32-bit elements; how exact they have to be, the bound alone decides.
A program may use at most 64 MiB of HBM per device.

v0:
```python
import jax
import jax.numpy as jnp
from jax import lax
from jax.sharding import PartitionSpec as P

PRECISE = lax.Precision.HIGHEST


def extended(block, sides, width):
    for axis, dim in sides:
        count = lax.axis_size(axis)
        forward = [(i, i + 1) for i in range(count - 1)]
        forward.append((count - 1, 0))
        backward = [(target, source) for source, target in forward]
        low = lax.ppermute(
            lax.slice_in_dim(block, block.shape[dim] - width, None, axis=dim), axis, forward
        )
        high = lax.ppermute(lax.slice_in_dim(block, 0, width, axis=dim), axis, backward)
        block = jnp.concatenate([low, block, high], axis=dim)
    return block


def neighbour_offset(sublattice, offset_id):
    if offset_id < 8:
        corner_bits = (offset_id >> 2 & 1, offset_id >> 1 & 1, offset_id & 1)
        if sublattice == 0:
            return ((-corner_bits[0], -corner_bits[1], -corner_bits[2]), 1)
        return (corner_bits, 0)
    axis_id = (offset_id - 8) // 2
    direction = 1 if (offset_id - 8) % 2 == 0 else -1
    displacement = tuple((direction if axis_number == axis_id else 0 for axis_number in range(3)))
    return (displacement, sublattice)


def offset_blocks(pair_blocks, slot_map):
    result = []
    for offset_id in range(14):
        chosen = slot_map[None, None] == offset_id
        result.append(jnp.sum(jnp.where(chosen, pair_blocks, jnp.float32(0.0)), axis=2))
    return result


def onsite_blocks(blocks):
    result = []
    for sublattice in range(2):
        onsite = jnp.zeros(blocks[0].shape[:2] + blocks[0].shape[3:], jnp.float32)
        for offset_id in range(14):
            coupling = blocks[offset_id][:, :, sublattice]
            onsite = onsite + 0.5 * (coupling + jnp.swapaxes(coupling, 0, 1))
        result.append(onsite)
    return result


def apply_hessian(vectors, blocks, onsite):
    padded = extended(vectors, (("gx", 3), ("gy", 4), ("gz", 5)), 1)
    size_x, size_y, size_z = (vectors.shape[3], vectors.shape[4], vectors.shape[5])
    outputs = []
    for sublattice in range(2):
        summed = jnp.zeros(vectors.shape[:2] + vectors.shape[3:], jnp.float32)
        for offset_id in range(14):
            displacement, source = neighbour_offset(sublattice, offset_id)
            start_x = 1 + displacement[0]
            start_y = 1 + displacement[1]
            start_z = 1 + displacement[2]
            neighbour = padded[
                :,
                :,
                source,
                start_x : start_x + size_x,
                start_y : start_y + size_y,
                start_z : start_z + size_z,
            ]
            coupling = blocks[offset_id][:, :, sublattice]
            summed = summed + jnp.sum(coupling[None] * neighbour[:, None], axis=2)
        summed = summed - jnp.sum(
            onsite[sublattice][None] * vectors[:, None, :, sublattice], axis=2
        )
        outputs.append(summed)
    return jnp.stack(outputs, axis=2)


def local_gram(left, right):
    left_flat = left.reshape(left.shape[0], -1)
    right_flat = right.reshape(right.shape[0], -1)
    return lax.dot_general(left_flat, right_flat, (((1,), (1,)), ((), ())), precision=PRECISE)


def combine(matrix, vectors):
    flat = vectors.reshape(vectors.shape[0], -1)
    return jnp.dot(matrix, flat, precision=PRECISE).reshape(vectors.shape)


def inverse_factor(gram_matrix):
    lower = jnp.linalg.cholesky(gram_matrix)
    identity = jnp.eye(gram_matrix.shape[0], dtype=gram_matrix.dtype)
    inverse = jax.scipy.linalg.solve_triangular(lower, identity, lower=True)
    return (lower, inverse)


def lanczos_step(basis, image, previous, coupling_prev, row_count):
    alpha = lax.psum(local_gram(image, basis), ("gx", "gy", "gz")) / row_count
    residual = image - combine(alpha, basis)
    if previous is not None:
        residual = residual - combine(coupling_prev.T, previous)
    residual_gram = lax.psum(local_gram(residual, residual), ("gx", "gy", "gz")) / row_count
    return (alpha, residual, residual_gram)


def local(start_block, pair_blocks, slot_map):
    device_count = lax.axis_size("gx") * lax.axis_size("gy") * lax.axis_size("gz")
    row_count = start_block[0].size * device_count
    blocks = offset_blocks(pair_blocks, slot_map)
    onsite = onsite_blocks(blocks)
    start_gram = lax.psum(local_gram(start_block, start_block), ("gx", "gy", "gz")) / row_count
    lower0, inverse0 = inverse_factor(start_gram)
    basis1 = combine(inverse0, start_block)
    image1 = apply_hessian(basis1, blocks, onsite)
    alpha1, residual1, gram_first = lanczos_step(basis1, image1, None, None, row_count)
    beta1, inverse1 = inverse_factor(gram_first)
    basis2 = combine(inverse1, residual1)
    image2 = apply_hessian(basis2, blocks, onsite)
    alpha2, residual2, gram_second = lanczos_step(basis2, image2, basis1, beta1, row_count)
    beta2, inverse2 = inverse_factor(gram_second)
    basis3 = combine(inverse2, residual2)
    return (alpha1, alpha2, beta1, beta2, basis3)


def solution(mesh):
    in_specs = (
        P(None, None, None, "gx", "gy", "gz"),
        P(None, None, None, None, "gx", "gy", "gz"),
        P(None, None, "gx", "gy", "gz"),
    )
    out_specs = (P(), P(), P(), P(), P(None, None, None, "gx", "gy", "gz"))
    return jax.shard_map(local, mesh=mesh, in_specs=in_specs, out_specs=out_specs, check_vma=False)
```

profile of v0, /device:TPU:1, one launch (start us, length us, event | category | flops | bytes accessed | tf_op | source)
XLA Modules:
  0.0 522.5 jit_solution(3226206658296597986)
XLA Ops:
  1.8 1.6 convolution_bitcast_fusion.2
  3.4 81.5 %psum.35 = f32[32,32]{0,1:T(8,128)S(1)} all-reduce(f32[32,32]{0,1:T(8,128)S(1)} %convolution_bitcast_fusion.2), channel_id=1, replica_groups=mesh['gx'=8,'gy'=4,'gz'=8] {'gx','gy','gz'}, use_global_device_ids=true, to_apply=%region_1.2 | all-reduce | flops 1024 | bytes 8192 | tf_op jit(solution)/shard_map/psum | solution.py:114
  85.0 2.9 cholesky.59
  89.3 2.4 custom-call.7
  94.1 2.5 select_reduce_fusion.13
  106.4 2.7 collective-permute-start.3
  113.4 6.9 %collective-permute-done.3 = f32[32,3,2,3,1,128]{5,0,4,3,2,1:T(8,128)S(1)} collective-permute-done((f32[32,3,2,3,1,128]{5,0,4,3,2,1:T(8,128)S(1)}, f32[32,3,2,3,1,128]{5,0,4,3,2,1:T(8,128)S(1)}, u32[]{:S(2)}, u32[]{:S(2)}) %collective-permute-start.3) | collective-permute-done | bytes 294944 | tf_op jit(solution)/shard_map/ppermute | solution.py:18
  121.2 1.8 fusion.52
  123.1 2.8 copy.507
  125.9 5.6 %collective-permute-start.5 = (f32[32,3,2,3,6,1]{0,2,5,4,3,1:T(2,128)}, f32[32,3,2,3,6,1]{0,2,5,4,3,1:T(2,128)}, u32[]{:S(2)}, u32[]{:S(2)}) collective-permute-start(f32[32,3,2,3,6,1]{0,2,5,4,3,1:T(2,128)} %copy.507), channel_id=1, source_target_pairs={{1,0},{2,1},{3,2},{4,3},{5,4},{6,5},{7,6},{0,7},{9,8},{10,9},{11,1... | collective-permute-start | bytes 41480 | tf_op jit(solution)/shard_map/ppermute | solution.py:18
  132.8 1.7 multiply_reduce_fusion.36
  134.5 2.7 copy.419
  137.2 5.0 collective-permute-done.4
  151.0 74.3 %psum.36 = f32[32,32]{0,1:T(8,128)S(1)} all-reduce(f32[32,32]{0,1:T(8,128)S(1)} %fusion.56), channel_id=1, replica_groups=mesh['gx'=8,'gy'=4,'gz'=8] {'gx','gy','gz'}, use_global_device_ids=true, to_apply=%region_47.50 | all-reduce | flops 1024 | bytes 8192 | tf_op jit(solution)/shard_map/psum | solution.py:101
  226.4 73.7 %psum.37 = f32[32,32]{0,1:T(8,128)S(1)} all-reduce(f32[32,32]{0,1:T(8,128)S(1)} %fusion.57), channel_id=1, replica_groups=mesh['gx'=8,'gy'=4,'gz'=8] {'gx','gy','gz'}, use_global_device_ids=true, to_apply=%region_48.51 | all-reduce | flops 1024 | bytes 8192 | tf_op jit(solution)/shard_map/psum | solution.py:105
  300.2 2.9 cholesky.70
  304.4 2.4 custom-call.8
  311.7 2.2 collective-permute-done.6
  314.0 2.6 collective-permute-done.7
  317.7 2.4 collective-permute-start.9
  322.6 4.1 collective-permute-done.8
  326.7 5.3 %collective-permute-done.9 = f32[32,3,2,3,1,128]{5,0,4,3,2,1:T(8,128)S(1)} collective-permute-done((f32[32,3,2,3,1,128]{5,0,4,3,2,1:T(8,128)S(1)}, f32[32,3,2,3,1,128]{5,0,4,3,2,1:T(8,128)S(1)}, u32[]{:S(2)}, u32[]{:S(2)}) %collective-permute-start.9) | collective-permute-done | bytes 294944 | tf_op jit(solution)/shard_map/ppermute | solution.py:18
  332.9 1.8 fusion.51
  334.8 2.8 copy.509
  337.6 4.7 collective-permute-start.11
  345.7 1.5 copy.488
  347.2 2.2 maximum_bitcast_fusion.4
  350.4 4.6 collective-permute-done.10
  363.7 73.7 %psum.38 = f32[32,32]{0,1:T(8,128)S(1)} all-reduce(f32[32,32]{0,1:T(8,128)S(1)} %fusion.59), channel_id=1, replica_groups=mesh['gx'=8,'gy'=4,'gz'=8] {'gx','gy','gz'}, use_global_device_ids=true, to_apply=%region_79.82 | all-reduce | flops 1024 | bytes 8192 | tf_op jit(solution)/shard_map/psum | solution.py:101
  439.1 73.7 %psum.39 = f32[32,32]{0,1:T(8,128)S(1)} all-reduce(f32[32,32]{0,1:T(8,128)S(1)} %fusion.60), channel_id=1, replica_groups=mesh['gx'=8,'gy'=4,'gz'=8] {'gx','gy','gz'}, use_global_device_ids=true, to_apply=%region_80.83 | all-reduce | flops 1024 | bytes 8192 | tf_op jit(solution)/shard_map/psum | solution.py:105
  512.8 2.9 cholesky.81
  517.6 2.4 custom-call.9
  (353 shorter events, 59.6 us)
Async XLA Ops:
  3.4 90.4 %copy-start.95 = (s32[16,2,1,4,128]{4,3,2,1,0:T(4,128)S(1)}, s32[16,2,1,4,128]{4,3,2,1,0:T(4,128)}, u32[]{:S(2)}) copy-start(s32[16,2,1,4,128]{4,3,2,1,0:T(4,128)} %param.8) | copy-start | bytes 196612
  88.6 5.5 %copy-start.35 = (f32[3,3,16,2,1,4,128]{6,5,4,3,2,1,0:T(4,128)S(1)}, f32[3,3,16,2,1,4,128]{6,5,4,3,2,1,0:T(4,128)}, u32[]{:S(2)}) copy-start(f32[3,3,16,2,1,4,128]{6,5,4,3,2,1,0:T(4,128)} %param.7) | copy-start | bytes 1769476
  92.8 12.8 %collective-permute-start = (f32[32,3,2,1,4,128]{5,0,4,3,2,1:T(8,128)S(1)}, f32[32,3,2,1,4,128]{5,0,4,3,2,1:T(8,128)S(1)}, u32[]{:S(2)}, u32[]{:S(2)}) collective-permute-start(f32[32,3,2,1,4,128]{5,0,4,3,2,1:T(8,128)S(1)} %copy.391), channel_id=1, source_target_pairs={{0,32},{32,64},{64,96},{96,128},{128,160},{160,192},{192,224},{224... | collective-permute-start | bytes 1179656 | tf_op jit(solution)/shard_map/ppermute | solution.py:15
  92.8 12.9 %collective-permute-start.1 = (f32[32,3,2,1,4,128]{5,0,4,3,2,1:T(8,128)S(1)}, f32[32,3,2,1,4,128]{5,0,4,3,2,1:T(8,128)S(1)}, u32[]{:S(2)}, u32[]{:S(2)}) collective-permute-start(f32[32,3,2,1,4,128]{5,0,4,3,2,1:T(8,128)S(1)} %copy.391), channel_id=1, source_target_pairs={{32,0},{64,32},{96,64},{128,96},{160,128},{192,160},{224,192},{0,2... | collective-permute-start | bytes 1179656 | tf_op jit(solution)/shard_map/ppermute | solution.py:18
  99.9 10.0 %copy-start.84 = (f32[3,3,4,128]{3,2,0,1:T(4,128)}, f32[3,3,4,128]{3,2,0,1:T(4,128)S(1)}, u32[]{:S(2)}) copy-start(f32[3,3,4,128]{3,2,0,1:T(4,128)S(1)} %get-tuple-element.159) | copy-start | bytes 55300
  99.9 10.7 %copy-start.82 = (f32[3,3,4,128]{3,2,0,1:T(4,128)}, f32[3,3,4,128]{3,2,0,1:T(4,128)S(1)}, u32[]{:S(2)}) copy-start(f32[3,3,4,128]{3,2,0,1:T(4,128)S(1)} %get-tuple-element.162) | copy-start | bytes 55300
  100.5 10.9 %copy-start.80 = (f32[3,3,4,128]{3,2,0,1:T(4,128)}, f32[3,3,4,128]{3,2,0,1:T(4,128)S(1)}, u32[]{:S(2)}) copy-start(f32[3,3,4,128]{3,2,0,1:T(4,128)S(1)} %get-tuple-element.194) | copy-start | bytes 55300
  102.5 8.1 %copy-start.88 = (f32[3,3,4,128]{3,2,0,1:T(4,128)}, f32[3,3,4,128]{3,2,0,1:T(4,128)S(1)}, u32[]{:S(2)}) copy-start(f32[3,3,4,128]{3,2,0,1:T(4,128)S(1)} %get-tuple-element.190) | copy-start | bytes 55300
  102.5 9.0 %copy-start.86 = (f32[3,3,4,128]{3,2,0,1:T(4,128)}, f32[3,3,4,128]{3,2,0,1:T(4,128)S(1)}, u32[]{:S(2)}) copy-start(f32[3,3,4,128]{3,2,0,1:T(4,128)S(1)} %get-tuple-element.189) | copy-start | bytes 55300
  105.8 7.6 %collective-permute-start.2 = (f32[32,3,2,3,1,128]{5,0,4,3,2,1:T(8,128)S(1)}, f32[32,3,2,3,1,128]{5,0,4,3,2,1:T(8,128)S(1)}, u32[]{:S(2)}, u32[]{:S(2)}) collective-permute-start(f32[32,3,2,3,1,128]{5,0,4,3,2,1:T(8,128)S(1)} %get-tuple-element.115), channel_id=1, source_target_pairs={{0,8},{8,16},{16,24},{24,0},{1,9},{9,17},{17,25},{25,1},{2,10},{10... | collective-permute-start | bytes 884744 | tf_op jit(solution)/shard_map/ppermute | solution.py:15
  106.4 13.9 %collective-permute-start.3 = (f32[32,3,2,3,1,128]{5,0,4,3,2,1:T(8,128)S(1)}, f32[32,3,2,3,1,128]{5,0,4,3,2,1:T(8,128)S(1)}, u32[]{:S(2)}, u32[]{:S(2)}) collective-permute-start(f32[32,3,2,3,1,128]{5,0,4,3,2,1:T(8,128)S(1)} %get-tuple-element.116), channel_id=1, source_target_pairs={{8,0},{16,8},{24,16},{0,24},{9,1},{17,9},{25,17},{1,25},{10,2},{18... | collective-permute-start | bytes 884744 | tf_op jit(solution)/shard_map/ppermute | solution.py:18
  113.4 6.9 %copy-start.8 = (f32[32,3,2,3,1,128]{5,0,4,3,2,1:T(8,128)}, f32[32,3,2,3,1,128]{5,0,4,3,2,1:T(8,128)S(1)}, u32[]{:S(2)}) copy-start(f32[32,3,2,3,1,128]{5,0,4,3,2,1:T(8,128)S(1)} %collective-permute-done.2) | copy-start | bytes 884740
  125.9 8.6 %collective-permute-start.5 = (f32[32,3,2,3,6,1]{0,2,5,4,3,1:T(2,128)}, f32[32,3,2,3,6,1]{0,2,5,4,3,1:T(2,128)}, u32[]{:S(2)}, u32[]{:S(2)}) collective-permute-start(f32[32,3,2,3,6,1]{0,2,5,4,3,1:T(2,128)} %copy.507), channel_id=1, source_target_pairs={{1,0},{2,1},{3,2},{4,3},{5,4},{6,5},{7,6},{0,7},{9,8},{10,9},{11,1... | collective-permute-start | bytes 41480 | tf_op jit(solution)/shard_map/ppermute | solution.py:18
  132.8 9.4 %collective-permute-start.4 = (f32[32,3,2,3,6,1]{0,2,5,4,3,1:T(2,128)}, f32[32,3,2,3,6,1]{0,2,5,4,3,1:T(2,128)}, u32[]{:S(2)}, u32[]{:S(2)}) collective-permute-start(f32[32,3,2,3,6,1]{0,2,5,4,3,1:T(2,128)} %copy.506), channel_id=1, source_target_pairs={{0,1},{1,2},{2,3},{3,4},{4,5},{5,6},{6,7},{7,0},{8,9},{9,10},{10,1... | collective-permute-start | bytes 41480 | tf_op jit(solution)/shard_map/ppermute | solution.py:15
  304.4 133.4 %copy-start.94 = (f32[32,32]{1,0:T(8,128)}, f32[32,32]{1,0:T(8,128)S(1)}, u32[]{:S(2)}) copy-start(f32[32,32]{1,0:T(8,128)S(1)} %get-tuple-element.76) | copy-start | bytes 12292
  307.6 2.5 copy-start.2
  307.6 2.5 copy-start.39
  307.6 2.5 copy-start.91
  307.9 5.9 %collective-permute-start.6 = (f32[32,3,2,1,4,128]{5,0,4,3,2,1:T(8,128)S(1)}, f32[32,3,2,1,4,128]{5,0,4,3,2,1:T(8,128)S(1)}, u32[]{:S(2)}, u32[]{:S(2)}) collective-permute-start(f32[32,3,2,1,4,128]{5,0,4,3,2,1:T(8,128)S(1)} %copy.482), channel_id=1, source_target_pairs={{0,32},{32,64},{64,96},{96,128},{128,160},{160,192},{192,224},{224... | collective-permute-start | bytes 1179656 | tf_op jit(solution)/shard_map/ppermute | solution.py:15
  309.1 7.5 %collective-permute-start.7 = (f32[32,3,2,1,4,128]{5,0,4,3,2,1:T(8,128)S(1)}, f32[32,3,2,1,4,128]{5,0,4,3,2,1:T(8,128)S(1)}, u32[]{:S(2)}, u32[]{:S(2)}) collective-permute-start(f32[32,3,2,1,4,128]{5,0,4,3,2,1:T(8,128)S(1)} %copy.482), channel_id=1, source_target_pairs={{32,0},{64,32},{96,64},{128,96},{160,128},{192,160},{224,192},{0,2... | collective-permute-start | bytes 1179656 | tf_op jit(solution)/shard_map/ppermute | solution.py:18
  314.0 6.2 %copy-start.85 = (f32[3,3,4,128]{3,2,0,1:T(4,128)S(1)}, f32[3,3,4,128]{3,2,0,1:T(4,128)}, u32[]{:S(2)}) copy-start(f32[3,3,4,128]{3,2,0,1:T(4,128)} %copy-done.84) | copy-start | bytes 55300
  316.7 4.2 copy-start.83
  316.7 4.2 copy-start.89
  316.7 5.1 copy-start.81
  316.7 5.1 copy-start.87
  316.7 10.0 %collective-permute-start.8 = (f32[32,3,2,3,1,128]{5,0,4,3,2,1:T(8,128)S(1)}, f32[32,3,2,3,1,128]{5,0,4,3,2,1:T(8,128)S(1)}, u32[]{:S(2)}, u32[]{:S(2)}) collective-permute-start(f32[32,3,2,3,1,128]{5,0,4,3,2,1:T(8,128)S(1)} %get-tuple-element.113), channel_id=1, source_target_pairs={{0,8},{8,16},{16,24},{24,0},{1,9},{9,17},{17,25},{25,1},{2,10},{10... | collective-permute-start | bytes 884744 | tf_op jit(solution)/shard_map/ppermute | solution.py:15
  317.7 14.3 %collective-permute-start.9 = (f32[32,3,2,3,1,128]{5,0,4,3,2,1:T(8,128)S(1)}, f32[32,3,2,3,1,128]{5,0,4,3,2,1:T(8,128)S(1)}, u32[]{:S(2)}, u32[]{:S(2)}) collective-permute-start(f32[32,3,2,3,1,128]{5,0,4,3,2,1:T(8,128)S(1)} %get-tuple-element.114), channel_id=1, source_target_pairs={{8,0},{16,8},{24,16},{0,24},{9,1},{17,9},{25,17},{1,25},{10,2},{18... | collective-permute-start | bytes 884744 | tf_op jit(solution)/shard_map/ppermute | solution.py:18
  326.7 5.3 %copy-start.4 = (f32[32,3,2,3,1,128]{5,0,4,3,2,1:T(8,128)}, f32[32,3,2,3,1,128]{5,0,4,3,2,1:T(8,128)S(1)}, u32[]{:S(2)}) copy-start(f32[32,3,2,3,1,128]{5,0,4,3,2,1:T(8,128)S(1)} %collective-permute-done.8) | copy-start | bytes 884740
  337.6 8.1 %collective-permute-start.11 = (f32[32,3,2,3,6,1]{0,2,5,4,3,1:T(2,128)}, f32[32,3,2,3,6,1]{0,2,5,4,3,1:T(2,128)}, u32[]{:S(2)}, u32[]{:S(2)}) collective-permute-start(f32[32,3,2,3,6,1]{0,2,5,4,3,1:T(2,128)} %copy.509), channel_id=1, source_target_pairs={{1,0},{2,1},{3,2},{4,3},{5,4},{6,5},{7,6},{0,7},{9,8},{10,9},{11,1... | collective-permute-start | bytes 41480 | tf_op jit(solution)/shard_map/ppermute | solution.py:18
  345.0 9.9 %collective-permute-start.10 = (f32[32,3,2,3,6,1]{0,2,5,4,3,1:T(2,128)}, f32[32,3,2,3,6,1]{0,2,5,4,3,1:T(2,128)}, u32[]{:S(2)}, u32[]{:S(2)}) collective-permute-start(f32[32,3,2,3,6,1]{0,2,5,4,3,1:T(2,128)} %copy.508), channel_id=1, source_target_pairs={{0,1},{1,2},{2,3},{3,4},{4,5},{5,6},{6,7},{7,0},{8,9},{9,10},{10,1... | collective-permute-start | bytes 41480 | tf_op jit(solution)/shard_map/ppermute | solution.py:15
  347.2 2.2 copy-start.1
  347.2 2.2 copy-start.59
  (76 other events, 85.8 us)
where the time goes:
time: 524 us; the launch traced here: 522 us
  blocking collectives  377 us (72%)
  other arithmetic  45.5 us (9%)
  local copies, waits for them, and re-layouts  39 us (7%)
  waiting for transfers between devices  31.8 us (6%)
  starting transfers between devices  19.9 us (4%)
  matrix products  7.11 us (1%)
    psum x2, blocking collectives, lanczos_step(): alpha = lax.psum(local_gram(image, basis), ('gx', 'gy', 'gz')) / row_count  148 us
    psum x2, blocking collectives, lanczos_step(): lax.psum(local_gram(residual, residual), ('gx', 'gy', 'gz')) / row_count  147 us
    psum x1, blocking collectives, local(): lax.psum(local_gram(start_block, start_block), ('gx', 'gy', 'gz'))  81.5 us
    unnamed x203, local copies, waits for them, and re-layouts  17 us
    ppermute x6, waiting for transfers between devices, extended(): lax.ppermute(lax.slice_in_dim(block, block.shape[dim] - width, None, axis...  17 us
    ppermute x6, starting transfers between devices, extended(): lax.ppermute(lax.slice_in_dim(block, 0, width, axis=dim), axis, backward)  16.3 us
    ppermute x6, waiting for transfers between devices, extended(): lax.ppermute(lax.slice_in_dim(block, 0, width, axis=dim), axis, backward)  14.8 us
    reduce_sum x42, other arithmetic, apply_hessian(): summed = summed + jnp.sum(coupling[None] * neighbour[:, None], axis=2)  12.5 us
  transfers between devices with their start and end apart: 12, of which 8 were waited for; matrix products, arithmetic and copies ran while one was open for 6% of the time, Pallas kernels for 0%

commit v1 on v0

--- a/solution.py
+++ b/solution.py
@@ -102,7 +102,13 @@
     residual = image - combine(alpha, basis)
     if previous is not None:
         residual = residual - combine(coupling_prev.T, previous)
-    residual_gram = lax.psum(local_gram(residual, residual), ("gx", "gy", "gz")) / row_count
+
+    def rest_slabs_now(sample, along_axis):
+        newest = lax.all_gather(sample, along_axis)
+        e_next = jnp.sum(newest, 0)
+        return e_next
+
+    residual_gram = rest_slabs_now(local_gram(residual, residual), ("gx", "gy", "gz")) / row_count
     return (alpha, residual, residual_gram)
 
 

time: 524 us -> 1810 us (3.45)
  waiting for transfers between devices: 31.8 us -> 1430 us
  blocking collectives: 377 us -> 234 us
    all_gather x0 -> x2, waiting for transfers between devices: none -> 1400 us  [rest_slabs_now(): newest = lax.all_gather(sample, along_axis)]
    psum x2 -> x0, blocking collectives: 147 us -> none  [lanczos_step(): lax.psum(local_gram(residual, residual), ('gx', 'gy', 'gz')) / row_count]
  transfers between devices with their start and end apart: 12 -> 14, of which waited for: 8 -> 9; matrix products, arithmetic and copies ran while one was open for 6% -> 2% of each run, Pallas kernels for 0% -> 0%
where the time goes in v1:
time: 1810 us; the launch traced here: 1800 us
  waiting for transfers between devices  1430 us (79%)
  blocking collectives  234 us (13%)
  other arithmetic  51.2 us (3%)
  local copies, waits for them, and re-layouts  39.1 us (2%)
  starting transfers between devices  25.8 us (1%)
    all_gather x2, waiting for transfers between devices, rest_slabs_now(): newest = lax.all_gather(sample, along_axis)  1400 us
    psum x2, blocking collectives, lanczos_step(): alpha = lax.psum(local_gram(image, basis), ('gx', 'gy', 'gz')) / row_count  152 us
    psum x1, blocking collectives, local(): lax.psum(local_gram(start_block, start_block), ('gx', 'gy', 'gz'))  81.5 us
  transfers between devices with their start and end apart: 14, of which 9 were waited for; matrix products, arithmetic and copies ran while one was open for 2% of the time, Pallas kernels for 0%

profile of v1, /device:TPU:1, one launch (start us, length us, event | category | flops | bytes accessed | tf_op | source)
XLA Modules:
  0.0 1803.2 jit_solution(11848156598074382441)
XLA Ops:
  10.0 81.5 %psum.21 = f32[32,32]{0,1:T(8,128)S(1)} all-reduce(f32[32,32]{0,1:T(8,128)S(1)} %convolution_bitcast_fusion.2), channel_id=1, replica_groups=mesh['gx'=8,'gy'=4,'gz'=8] {'gx','gy','gz'}, use_global_device_ids=true, to_apply=%region_1.2 | all-reduce | flops 1024 | bytes 8192 | tf_op jit(solution)/shard_map/psum | solution.py:120
  91.6 2.9 cholesky.59
  95.9 2.4 custom-call.7
  100.7 2.5 select_reduce_fusion.13
  113.0 2.7 collective-permute-start.3
  120.0 6.9 collective-permute-done.3
  127.8 1.8 fusion.52
  129.7 2.8 copy.503
  132.4 5.6 collective-permute-start.5
  139.4 1.7 multiply_reduce_fusion.36
  141.0 2.7 copy.417
  143.8 5.0 collective-permute-done.4
  157.6 74.4 %psum.22 = f32[32,32]{0,1:T(8,128)S(1)} all-reduce(f32[32,32]{0,1:T(8,128)S(1)} %fusion.56), channel_id=1, replica_groups=mesh['gx'=8,'gy'=4,'gz'=8] {'gx','gy','gz'}, use_global_device_ids=true, to_apply=%region_47.50 | all-reduce | flops 1024 | bytes 8192 | tf_op jit(solution)/shard_map/psum | solution.py:101
  233.7 703.0 %all-gather.5.cloned.1.call-done = f32[8192,32]{1,0:T(8,128)} async-done(((f32[32,32]{1,0:T(8,128)}), f32[8192,32]{1,0:T(8,128)}) %all-gather.5.cloned.1.call-update) | async-done | bytes 1048592 | tf_op jit(solution)/shard_map/all_gather | solution.py:107
  936.7 2.5 reduce_sum.870
  939.4 2.9 cholesky.70
  944.2 2.4 custom-call.8
  950.4 2.0 collective-permute-done.6
  952.6 2.7 collective-permute-done.7
  955.4 3.1 collective-permute-start.8
  958.5 4.7 collective-permute-start.9
  965.7 3.3 collective-permute-done.8
  969.0 3.5 collective-permute-done.9
  973.4 1.8 fusion.51
  975.3 2.8 copy.505
  980.8 7.0 collective-permute-start.10
  989.4 2.2 maximum_bitcast_fusion.4
  1001.3 78.0 %psum.23 = f32[32,32]{0,1:T(8,128)S(1)} all-reduce(f32[32,32]{0,1:T(8,128)S(1)} %fusion.59), channel_id=1, replica_groups=mesh['gx'=8,'gy'=4,'gz'=8] {'gx','gy','gz'}, use_global_device_ids=true, to_apply=%region_79.82 | all-reduce | flops 1024 | bytes 8192 | tf_op jit(solution)/shard_map/psum | solution.py:101
  1083.0 701.6 %all-gather.7.cloned.1.call-done = f32[8192,32]{1,0:T(8,128)} async-done(((f32[32,32]{1,0:T(8,128)}), f32[8192,32]{1,0:T(8,128)}) %all-gather.7.cloned.1.call-update) | async-done | bytes 1048592 | tf_op jit(solution)/shard_map/all_gather | solution.py:107
  1784.6 2.5 reduce_sum.921
  1787.3 2.9 cholesky.81
  1792.1 2.4 custom-call.9
  (361 shorter events, 62.9 us)
Async XLA Ops:
  7.2 929.5 %all-gather.5.cloned.1.call-start = ((), (), s32[]{:S(2)}) async-start(), calls=%async_computation | async-start | bytes 4210688 | tf_op jit(solution)/shard_map/all_gather | solution.py:107
  10.0 90.4 %copy-start.95 = (s32[16,2,1,4,128]{4,3,2,1,0:T(4,128)S(1)}, s32[16,2,1,4,128]{4,3,2,1,0:T(4,128)}, u32[]{:S(2)}) copy-start(s32[16,2,1,4,128]{4,3,2,1,0:T(4,128)} %param.8) | copy-start | bytes 196612
  95.2 5.5 copy-start.35
  99.3 12.8 collective-permute-start
  99.4 12.9 collective-permute-start.1
  106.5 10.0 copy-start.84
  106.5 10.7 copy-start.82
  107.1 10.9 copy-start.80
  109.0 8.1 copy-start.88
  109.1 9.0 copy-start.86
  112.4 7.6 collective-permute-start.2
  113.0 13.9 collective-permute-start.3
  120.0 6.9 copy-start.8
  132.4 8.6 collective-permute-start.5
  139.4 9.4 collective-permute-start.4
  233.6 1551.0 %all-gather.7.cloned.1.call-start = ((), (), s32[]{:S(2)}) async-start(), calls=%async_computation.1 | async-start | bytes 4210688 | tf_op jit(solution)/shard_map/all_gather | solution.py:107
  947.7 4.7 collective-permute-start.6
  947.7 7.5 collective-permute-start.7
  952.5 10.7 copy-start.85
  955.3 8.7 copy-start.83
  955.3 8.7 copy-start.89
  955.3 9.6 copy-start.81
  955.3 9.6 copy-start.87
  955.4 13.6 collective-permute-start.8
  958.5 14.0 collective-permute-start.9
  969.0 3.5 copy-start.4
  978.0 9.8 collective-permute-start.11
  980.8 11.7 collective-permute-start.10
  989.4 2.2 copy-start.1
  989.4 2.2 copy-start.59
  989.4 2.2 copy-start.63
  999.8 80.0 %copy-start.94 = (f32[32,32]{1,0:T(8,128)S(1)}, f32[32,32]{1,0:T(8,128)}, u32[]{:S(2)}) copy-start(f32[32,32]{1,0:T(8,128)} %get-tuple-element.76) | copy-start | bytes 12292
  (78 other events, 88.6 us)
Sparse Core Ops, SparseCore 0:
  233.7 702.8 all-gather.4
  1081.5 703.0 all-gather.6
